TPU v7x, 32 devices: a whole 2x2x4 slice. The times are simulated.
32 devices in a mesh: grp: 2 (over x), wave: 16 (over z, y, core).
Axes of the slice: x: 2, y: 2, z: 4, core: 2. Of those that a mesh axis runs over, the one named last changes fastest.
Arguments:
- north_rows: bfloat16 [2560, 128, 274], P(('grp', 'wave')), parts along dimension 0, may hold values from -6 to 6
- south_rows: bfloat16 [2560, 128, 274], P(('grp', 'wave')), parts along dimension 0, may hold values from -6 to 6
- lon_counts: int32 [1280], replicated, may hold values from 20 to 5148, as said below
- slot_wave: int32 [128], replicated, may hold values from 0 to 2559, as said below
- legendre: bfloat16 [128, 1280, 1280], P('wave'), may hold values from -0.15625 to 0.15625
- mode_rates: float32 [137], replicated, may hold values from 0.05 to 20
- to_modes: bfloat16 [137, 137], replicated, may hold values from -0.5 to 0.5
- from_modes: bfloat16 [137, 137], replicated, may hold values from -0.5 to 0.5
Outputs:
- spec_state: bfloat16 [256, 1280, 274], P(('grp', 'wave')), parts along dimension 0
- new_rows: bfloat16 [2560, 128, 274], P(('grp', 'wave')), parts along dimension 0
There are 2 independent parts, one for each index of `grp`. A program takes and returns all parts, laid end to end along the dimension named above; an argument that names none is the same for every part. Nothing has to cross between parts.
Inputs may be any that keep to these rules, and one draw needn't show every extreme that they name: Wavenumber m is present in latitude row j only if 2 m is below lon_counts[j]. `slot_wave`: distinct zonal wavenumbers.
All inputs are finite; a program needn't handle non-finite values.
Results may differ from a plain program's by a relative error of at most 0.0065.
Values may be sent and summed in bfloat16 or wider, within the bound.
A program may use at most 192 MiB of HBM per device.

v0:
```python
import jax
import jax.numpy as jnp
from jax import lax
from jax.sharding import PartitionSpec as P

NMAX = 2559


def vertical_step(direct, own_waves, mode_rates, to_modes, from_modes):
    slot_count, row_total, channels = direct.shape
    levels = to_modes.shape[0]
    modal_part = jnp.dot(direct.reshape(-1, levels), to_modes, preferred_element_type=jnp.float32)
    modal_part = modal_part.reshape(slot_count, row_total, 2, levels)
    degree = own_waves[:, None] + 2 * jnp.arange(row_total, dtype=jnp.int32)[None, :]
    degree_f = degree.astype(jnp.float32)
    scaled_degree = degree_f * (degree_f + 1.0) / float(NMAX * (NMAX + 1))
    divisor = 1.0 + mode_rates[None, None, None, :] * scaled_degree[:, :, None, None]
    scaled = (modal_part / divisor).astype(jnp.bfloat16).reshape(-1, levels)
    result = jnp.dot(scaled, from_modes, preferred_element_type=jnp.float32)
    result = result.reshape(slot_count, row_total, channels)
    return jnp.where((degree <= NMAX)[:, :, None], result, 0.0).astype(jnp.bfloat16)


def per_device(
    north_rows, south_rows, lon_counts, slot_wave, legendre, mode_rates, to_modes, from_modes
):
    lat_dev = north_rows.shape[0]
    slot_dev, row_total, lat_total = legendre.shape
    my_index = lax.axis_index("wave")
    own_waves = lax.dynamic_slice_in_dim(slot_wave, my_index * slot_dev, slot_dev)
    live_own = 2 * own_waves[None, :] < lon_counts[:, None]
    local_counts = lax.dynamic_slice_in_dim(lon_counts, my_index * lat_dev, lat_dev)
    live_here = 2 * slot_wave[None, :] < local_counts[:, None]
    summed = north_rows.astype(jnp.float32) + south_rows.astype(jnp.float32)
    sym_here = jnp.where(live_here[:, :, None], summed, 0.0).astype(jnp.bfloat16)
    columns = lax.all_to_all(sym_here, "wave", split_axis=1, concat_axis=0, tiled=True)
    direct = jnp.einsum(
        "snj,jsc->snc", legendre, columns, preferred_element_type=jnp.float32
    ).astype(jnp.bfloat16)
    spec_state = vertical_step(direct, own_waves, mode_rates, to_modes, from_modes)
    returned = jnp.einsum("snj,snc->jsc", legendre, spec_state, preferred_element_type=jnp.float32)
    returned = jnp.where(live_own[:, :, None], returned, 0.0).astype(jnp.bfloat16)
    new_rows = lax.all_to_all(returned, "wave", split_axis=0, concat_axis=1, tiled=True)
    return (spec_state, new_rows)


def solution(mesh):
    in_specs = (
        P(("grp", "wave"), None, None),
        P(("grp", "wave"), None, None),
        P(),
        P(),
        P("wave", None, None),
        P(),
        P(),
        P(),
    )
    out_specs = (P(("grp", "wave"), None, None), P(("grp", "wave"), None, None))
    return jax.shard_map(
        per_device, mesh=mesh, in_specs=in_specs, out_specs=out_specs, check_vma=False
    )
```

profile of v0, /device:TPU:15, one launch (start us, length us, event | category | flops | bytes accessed | tf_op | source)
XLA Modules:
  0.0 580.0 jit_solution(6979879642193113835)
XLA Ops:
  0.7 11.0 %copy.45 = bf16[80,128,274]{2,0,1:T(8,128)(2,1)} copy(bf16[80,128,274]{1,0,2:T(8,128)(2,1)} %param.9) | data formatting | bytes 11223040 | tf_op args[1]
  11.6 11.0 %copy.44 = bf16[80,128,274]{2,0,1:T(8,128)(2,1)} copy(bf16[80,128,274]{1,0,2:T(8,128)(2,1)} %param.8) | data formatting | bytes 11223040 | tf_op args[0]
  22.9 9.6 %select_convert_fusion.1 = bf16[80,128,274]{2,0,1:T(8,128)(2,1)} fusion(bf16[80,128,274]{2,0,1:T(8,128)(2,1)} %copy.45, bf16[80,128,274]{2,0,1:T(8,128)(2,1)} %copy.44, pred[80,128]{0,1:T(8,128)(4,1)S(1)} %broadcast_compare_fusion), kind=kLoop, calls=%fused_computation.1 | loop fusion | flops 14028800 | bytes 16844800 | tf_op jit(solution)/shard_map/convert_element_type | solution.py:35
  32.5 6.7 %all-to-all-start = ((bf16[80,128,274]{2,0,1:T(8,128)(2,1)}), bf16[80,128,274]{2,0,1:T(8,128)(2,1)}, u32[]{:S(2)}, u32[]{:S(2)}) async-start(bf16[80,128,274]{2,0,1:T(8,128)(2,1)} %select_convert_fusion.1), calls=%async_computation | async-start | bytes 15728640 | tf_op jit(solution)/shard_map/all_to_all | solution.py:36
  39.5 3.2 multiply_add_fusion
  42.7 167.6 %all-to-all-done = bf16[80,128,274]{2,0,1:T(8,128)(2,1)} async-done(((bf16[80,128,274]{2,0,1:T(8,128)(2,1)}), bf16[80,128,274]{2,0,1:T(8,128)(2,1)}, u32[]{:S(2)}, u32[]{:S(2)}) %all-to-all-start) | async-done | bytes 5611552 | tf_op jit(solution)/shard_map/all_to_all | solution.py:36
  210.3 14.5 %copy.65 = bf16[16,80,8,274]{1,0,3,2:T(8,128)(2,1)} copy(bf16[16,80,8,274]{3,1,2,0:T(8,128)(2,1)} %bitcast.2) | data formatting | bytes 11223040 | tf_op jit(solution)/shard_map/all_to_all | solution.py:36
  224.8 13.2 %reshape.146 = bf16[1280,8,274]{0,2,1:T(8,128)(2,1)} reshape(bf16[16,80,8,274]{1,0,3,2:T(8,128)(2,1)} %copy.65) | data formatting | bytes 11223040 | tf_op jit(solution)/shard_map/all_to_all | solution.py:36
  238.0 25.7 %convert_bitcast_fusion = bf16[8,1280,274]{1,2,0:T(8,128)(2,1)} fusion(bf16[1280,8,274]{0,2,1:T(8,128)(2,1)} %reshape.146, bf16[8,1280,1280]{2,1,0:T(8,128)(2,1)} %param.12), kind=kOutput, calls=%fused_computation.8 | convolution fusion | flops 7185551360 | bytes 37437440 | tf_op jit(solution)/shard_map/snj,jsc->snc/dot_general | solution.py:37
  263.7 3.7 copy.49
  267.4 6.4 %divide_convert_fusion = bf16[8,1280,2,137]{1,3,2,0:T(8,128)(2,1)} fusion(bf16[8,1280,2,137]{1,0,3,2:T(8,128)(2,1)S(1)} %bitcast.31, f32[8,1280,137]{1,2,0:T(8,128)} %multiply_add_fusion, bf16[137,137]{1,0:T(8,128)(2,1)S(1)} %copy-done), kind=kOutput, calls=%fused_computation.2 | convolution fusion | flops 774389760 | bytes 16872098 | tf_op jit(solution)/shard_map/dot_general | solution.py:12
  273.8 25.2 %copy.52 = bf16[8,1280,2,137]{3,2,1,0:T(2,128)(2,1)} copy(bf16[8,1280,2,137]{1,3,2,0:T(8,128)(2,1)} %divide_convert_fusion) | data formatting | bytes 11223040 | tf_op jit(solution)/shard_map/convert_element_type | solution.py:18
  299.1 18.9 %reshape.143 = bf16[20480,137]{1,0:T(8,128)(2,1)} reshape(bf16[8,1280,2,137]{3,2,1,0:T(2,128)(2,1)} %copy.52) | data formatting | bytes 11223040 | tf_op jit(solution)/shard_map/reshape | solution.py:18
  318.0 10.8 %fusion.4 = bf16[20480,137]{1,0:T(8,128)(2,1)} fusion(bf16[20480,137]{1,0:T(8,128)(2,1)} %reshape.143, bf16[137,137]{1,0:T(8,128)(2,1)S(1)} %copy-done.2), kind=kOutput, calls=%fused_computation.19 | convolution fusion | flops 768778240 | bytes 11260578 | tf_op jit(solution)/shard_map/dot_general | solution.py:19
  328.8 16.0 %reshape.144 = bf16[8,1280,274]{2,1,0:T(8,128)(2,1)} reshape(bf16[20480,137]{1,0:T(8,128)(2,1)} %fusion.4) | data formatting | bytes 11223040 | tf_op jit(solution)/shard_map/reshape | solution.py:20
  344.8 7.6 %select_convert_fusion = bf16[8,1280,274]{2,1,0:T(8,128)(2,1)} fusion(bf16[8,1280,274]{2,1,0:T(8,128)(2,1)} %reshape.144, pred[8,1280]{1,0:T(8,128)(4,1)S(1)} %add_compare_fusion), kind=kLoop, calls=%fused_computation | loop fusion | flops 2805760 | bytes 11233280 | tf_op jit(solution)/shard_map/convert_element_type | solution.py:21
  352.4 16.3 %fusion.5 = bf16[8,274,1280]{2,1,0:T(8,128)(2,1)} fusion(bf16[8,1280,274]{2,1,0:T(8,128)(2,1)} %select_convert_fusion, bf16[8,1280,1280]{2,1,0:T(8,128)(2,1)} %param.12), kind=kOutput, calls=%fused_computation.20 | convolution fusion | flops 7182745600 | bytes 37437440 | tf_op jit(solution)/shard_map/snj,snc->jsc/dot_general | solution.py:41
  368.7 6.5 %fusion = bf16[1280,8,274]{0,1,2:T(8,128)(2,1)} fusion(bf16[8,274,1280]{2,1,0:T(8,128)(2,1)} %fusion.5, pred[1280,8]{0,1:T(8,128)(4,1)S(1)} %broadcast_compare_fusion.1), kind=kLoop, calls=%fused_computation.4 | loop fusion | flops 2805760 | bytes 11233280 | tf_op jit(solution)/shard_map/convert_element_type | solution.py:42
  375.2 10.9 %copy.56 = bf16[1280,8,274]{2,1,0:T(8,128)(2,1)} copy(bf16[1280,8,274]{0,1,2:T(8,128)(2,1)} %fusion) | data formatting | bytes 11223040 | tf_op jit(solution)/shard_map/convert_element_type | solution.py:42
  386.2 4.8 all-to-all-start.1
  391.0 10.1 %copy.59 = bf16[8,1280,274]{1,0,2:T(8,128)(2,1)} copy(bf16[8,1280,274]{2,1,0:T(8,128)(2,1)} %select_convert_fusion) | data formatting | bytes 11223040
  401.0 161.1 %all-to-all-done.1 = bf16[1280,8,274]{2,1,0:T(8,128)(2,1)} async-done(((bf16[1280,8,274]{2,1,0:T(8,128)(2,1)}), bf16[1280,8,274]{2,1,0:T(8,128)(2,1)}, u32[]{:S(2)}, u32[]{:S(2)}) %all-to-all-start.1) | async-done | bytes 5611552 | tf_op jit(solution)/shard_map/all_to_all | solution.py:43
  562.1 7.9 %copy.74 = bf16[80,16,8,274]{3,2,1,0:T(8,128)(2,1)} copy(bf16[80,16,8,274]{3,2,0,1:T(8,128)(2,1)} %bitcast.9) | data formatting | bytes 11223040 | tf_op jit(solution)/shard_map/all_to_all | solution.py:43
  570.0 10.0 %copy.60 = bf16[80,128,274]{1,0,2:T(8,128)(2,1)} copy(bf16[80,128,274]{2,1,0:T(8,128)(2,1)} %bitcast.30) | data formatting | bytes 11223040
  (20 shorter events, 0.5 us)
Async XLA Ops:
  0.6 266.8 %copy-start = (bf16[137,137]{1,0:T(8,128)(2,1)S(1)}, bf16[137,137]{1,0:T(8,128)(2,1)}, u32[]{:S(2)}) copy-start(bf16[137,137]{1,0:T(8,128)(2,1)} %param.14) | copy-start | bytes 112618
  11.6 11.1 %copy-start.5 = (s32[128]{0:T(128)S(1)}, s32[128]{0:T(128)}, u32[]{:S(2)}) copy-start(s32[128]{0:T(128)} %param.11) | copy-start | bytes 1540
  11.6 11.1 %copy-start.3 = (s32[1280]{0:T(1024)S(1)}, s32[1280]{0:T(1024)}, u32[]{:S(2)}) copy-start(s32[1280]{0:T(1024)} %param.10) | copy-start | bytes 15364
  32.5 7.0 %copy-start.4 = (f32[137]{0:T(256)S(1)}, f32[137]{0:T(256)}, u32[]{:S(2)}) copy-start(f32[137]{0:T(256)} %param.13) | copy-start | bytes 1648
  32.5 177.8 %all-to-all-start = ((bf16[80,128,274]{2,0,1:T(8,128)(2,1)}), bf16[80,128,274]{2,0,1:T(8,128)(2,1)}, u32[]{:S(2)}, u32[]{:S(2)}) async-start(bf16[80,128,274]{2,0,1:T(8,128)(2,1)} %select_convert_fusion.1), calls=%async_computation | async-start | bytes 15728640 | tf_op jit(solution)/shard_map/all_to_all | solution.py:36
  299.1 18.9 %copy-start.2 = (bf16[137,137]{1,0:T(8,128)(2,1)S(1)}, bf16[137,137]{1,0:T(8,128)(2,1)}, u32[]{:S(2)}) copy-start(bf16[137,137]{1,0:T(8,128)(2,1)} %param.15) | copy-start | bytes 112618
  386.2 175.9 %all-to-all-start.1 = ((bf16[1280,8,274]{2,1,0:T(8,128)(2,1)}), bf16[1280,8,274]{2,1,0:T(8,128)(2,1)}, u32[]{:S(2)}, u32[]{:S(2)}) async-start(bf16[1280,8,274]{2,1,0:T(8,128)(2,1)} %copy.56), calls=%async_computation.1 | async-start | bytes 15728640 | tf_op jit(solution)/shard_map/all_to_all | solution.py:43
  562.1 17.9 %copy-start.1 = (bf16[137,137]{1,0:T(8,128)(2,1)S(1)}, bf16[137,137]{1,0:T(8,128)(2,1)}, u32[]{:S(2)}) copy-start(bf16[137,137]{1,0:T(8,128)(2,1)} %param.14) | copy-start | bytes 112618
where the time goes:
time: 584 us; the launch traced here: 580 us
  waiting for transfers between devices  329 us (56%)
  local copies, waits for them, and re-layouts  153 us (26%)
  matrix products  59.3 us (10%)
  other arithmetic  27.3 us (5%)
  starting transfers between devices  11.4 us (2%)
    all_to_all x1, waiting for transfers between devices, per_device(): lax.all_to_all(sym_here, 'wave', split_axis=1, concat_axis=0, tiled=True)  168 us
    all_to_all x1, waiting for transfers between devices, per_device(): lax.all_to_all(returned, 'wave', split_axis=0, concat_axis=1, tiled=True)  161 us
    unnamed x16, local copies, waits for them, and re-layouts  42.2 us
    all_to_all x2, local copies, waits for them, and re-layouts, per_device(): lax.all_to_all(sym_here, 'wave', split_axis=1, concat_axis=0, tiled=True)  27.8 us
    dot_general x1, matrix products, per_device(): jnp.einsum('snj,jsc->snc', legendre, columns, preferred_element_type=jnp....  25.7 us
    convert_element_type x1, local copies, waits for them, and re-layouts, vertical_step(): scaled = (modal_part / divisor).astype(jnp.bfloat16).reshape(-1, levels)  25.2 us
    reshape x1, local copies, waits for them, and re-layouts, vertical_step(): scaled = (modal_part / divisor).astype(jnp.bfloat16).reshape(-1, levels)  18.9 us
    dot_general x1, matrix products, per_device(): jnp.einsum('snj,snc->jsc', legendre, spec_state, preferred_element_type=j...  16.3 us
  transfers between devices with their start and end apart: 2, of which 2 were waited for; matrix products, arithmetic and copies ran while one was open for 2% of the time, Pallas kernels for 0%

commit v1 on v0

--- a/solution.py
+++ b/solution.py
@@ -40,7 +40,9 @@
     spec_state = vertical_step(direct, own_waves, mode_rates, to_modes, from_modes)
     returned = jnp.einsum("snj,snc->jsc", legendre, spec_state, preferred_element_type=jnp.float32)
     returned = jnp.where(live_own[:, :, None], returned, 0.0).astype(jnp.bfloat16)
-    new_rows = lax.all_to_all(returned, "wave", split_axis=0, concat_axis=1, tiled=True)
+    u_next = jnp.stack(jnp.split(returned, lax.axis_size("wave"), axis=0), axis=0)
+    s_next = lax.all_to_all(u_next, "wave", 0, 0)
+    new_rows = jnp.concatenate(s_next, axis=1)
     return (spec_state, new_rows)
 
 

time: 584 us -> 607 us (1.039)
  local copies, waits for them, and re-layouts: 153 us -> 182 us
    unnamed x16 -> x33, local copies, waits for them, and re-layouts: 42.2 us -> 66.9 us
    another operation x0 -> x2, local copies, waits for them, and re-layouts: none -> 15.5 us  [per_device(): jnp.stack(jnp.split(returned, lax.axis_size('wave'), axis=0), axis=0)]
    convert_element_type x1 -> x0, local copies, waits for them, and re-layouts: 10.9 us -> none  [per_device(): jnp.where(live_own[:, :, None], returned, 0.0).astype(jnp.bfloat16)]
    all_to_all x1 -> x0, local copies, waits for them, and re-layouts: 7.89 us -> none  [per_device(): lax.all_to_all(returned, 'wave', split_axis=0, concat_axis=1, tiled=True)]
    reshape x0 -> x1, local copies, waits for them, and re-layouts: none -> 7.88 us  [per_device(): new_rows = jnp.concatenate(s_next, axis=1)]
    convert_element_type x1 -> x0, other arithmetic: 6.5 us -> none  [per_device(): jnp.where(live_own[:, :, None], returned, 0.0).astype(jnp.bfloat16)]
where the time goes in v1:
time: 607 us; the launch traced here: 604 us
  waiting for transfers between devices  329 us (54%)
  local copies, waits for them, and re-layouts  182 us (30%)
  matrix products  59.3 us (10%)
  other arithmetic  21.5 us (4%)
  starting transfers between devices  11.4 us (2%)
    all_to_all x1, waiting for transfers between devices, per_device(): lax.all_to_all(sym_here, 'wave', split_axis=1, concat_axis=0, tiled=True)  168 us
    all_to_all x1, waiting for transfers between devices, per_device(): s_next = lax.all_to_all(u_next, 'wave', 0, 0)  161 us
    unnamed x33, local copies, waits for them, and re-layouts  66.9 us
    all_to_all x2, local copies, waits for them, and re-layouts, per_device(): lax.all_to_all(sym_here, 'wave', split_axis=1, concat_axis=0, tiled=True)  27.8 us
    dot_general x1, matrix products, per_device(): jnp.einsum('snj,jsc->snc', legendre, columns, preferred_element_type=jnp....  25.7 us
    convert_element_type x1, local copies, waits for them, and re-layouts, vertical_step(): scaled = (modal_part / divisor).astype(jnp.bfloat16).reshape(-1, levels)  25.2 us
    reshape x1, local copies, waits for them, and re-layouts, vertical_step(): scaled = (modal_part / divisor).astype(jnp.bfloat16).reshape(-1, levels)  18.9 us
    dot_general x1, matrix products, per_device(): jnp.einsum('snj,snc->jsc', legendre, spec_state, preferred_element_type=j...  16.4 us
  transfers between devices with their start and end apart: 2, of which 2 were waited for; matrix products, arithmetic and copies ran while one was open for 2% of the time, Pallas kernels for 0%

profile of v1, /device:TPU:15, one launch (start us, length us, event | category | flops | bytes accessed | tf_op | source)
XLA Modules:
  0.0 603.5 jit_solution(16521682510964045879)
XLA Ops:
  1.3 11.0 %copy.39 = bf16[80,128,274]{2,0,1:T(8,128)(2,1)} copy(bf16[80,128,274]{1,0,2:T(8,128)(2,1)} %param.8) | data formatting | bytes 11223040 | tf_op args[0]
  12.3 11.0 %copy.40 = bf16[80,128,274]{2,0,1:T(8,128)(2,1)} copy(bf16[80,128,274]{1,0,2:T(8,128)(2,1)} %param.9) | data formatting | bytes 11223040 | tf_op args[1]
  23.5 9.6 %select_convert_fusion.1 = bf16[80,128,274]{2,0,1:T(8,128)(2,1)} fusion(bf16[80,128,274]{2,0,1:T(8,128)(2,1)} %copy.40, bf16[80,128,274]{2,0,1:T(8,128)(2,1)} %copy.39, pred[80,128]{0,1:T(8,128)(4,1)S(1)} %broadcast_compare_fusion), kind=kLoop, calls=%fused_computation.1 | loop fusion | flops 14028800 | bytes 16844800 | tf_op jit(solution)/shard_map/convert_element_type | solution.py:35
  33.1 6.7 %all-to-all-start = ((bf16[80,128,274]{2,0,1:T(8,128)(2,1)}), bf16[80,128,274]{2,0,1:T(8,128)(2,1)}, u32[]{:S(2)}, u32[]{:S(2)}) async-start(bf16[80,128,274]{2,0,1:T(8,128)(2,1)} %select_convert_fusion.1), calls=%async_computation | async-start | bytes 15728640 | tf_op jit(solution)/shard_map/all_to_all | solution.py:36
  40.1 3.2 multiply_add_fusion
  43.3 167.6 %all-to-all-done = bf16[80,128,274]{2,0,1:T(8,128)(2,1)} async-done(((bf16[80,128,274]{2,0,1:T(8,128)(2,1)}), bf16[80,128,274]{2,0,1:T(8,128)(2,1)}, u32[]{:S(2)}, u32[]{:S(2)}) %all-to-all-start) | async-done | bytes 5611552 | tf_op jit(solution)/shard_map/all_to_all | solution.py:36
  210.9 14.5 %copy.58 = bf16[16,80,8,274]{1,0,3,2:T(8,128)(2,1)} copy(bf16[16,80,8,274]{3,1,2,0:T(8,128)(2,1)} %bitcast.2) | data formatting | bytes 11223040 | tf_op jit(solution)/shard_map/all_to_all | solution.py:36
  225.4 13.3 %reshape.154 = bf16[1280,8,274]{0,2,1:T(8,128)(2,1)} reshape(bf16[16,80,8,274]{1,0,3,2:T(8,128)(2,1)} %copy.58) | data formatting | bytes 11223040 | tf_op jit(solution)/shard_map/all_to_all | solution.py:36
  238.7 25.7 %convert_bitcast_fusion = bf16[8,1280,274]{1,2,0:T(8,128)(2,1)} fusion(bf16[1280,8,274]{0,2,1:T(8,128)(2,1)} %reshape.154, bf16[8,1280,1280]{2,1,0:T(8,128)(2,1)} %param.12), kind=kOutput, calls=%fused_computation.8 | convolution fusion | flops 7185551360 | bytes 37437440 | tf_op jit(solution)/shard_map/snj,jsc->snc/dot_general | solution.py:37
  264.3 3.7 copy.44
  268.0 6.5 %divide_convert_fusion = bf16[8,1280,2,137]{1,3,2,0:T(8,128)(2,1)} fusion(bf16[8,1280,2,137]{1,0,3,2:T(8,128)(2,1)S(1)} %bitcast.92, f32[8,1280,137]{1,2,0:T(8,128)} %multiply_add_fusion, bf16[137,137]{1,0:T(8,128)(2,1)S(1)} %copy-done), kind=kOutput, calls=%fused_computation.2 | convolution fusion | flops 774389760 | bytes 16872098 | tf_op jit(solution)/shard_map/dot_general | solution.py:12
  274.5 25.2 %copy.47 = bf16[8,1280,2,137]{3,2,1,0:T(2,128)(2,1)} copy(bf16[8,1280,2,137]{1,3,2,0:T(8,128)(2,1)} %divide_convert_fusion) | data formatting | bytes 11223040 | tf_op jit(solution)/shard_map/convert_element_type | solution.py:18
  299.7 18.9 %reshape.149 = bf16[20480,137]{1,0:T(8,128)(2,1)} reshape(bf16[8,1280,2,137]{3,2,1,0:T(2,128)(2,1)} %copy.47) | data formatting | bytes 11223040 | tf_op jit(solution)/shard_map/reshape | solution.py:18
  318.6 10.8 %fusion.20 = bf16[20480,137]{1,0:T(8,128)(2,1)} fusion(bf16[20480,137]{1,0:T(8,128)(2,1)} %reshape.149, bf16[137,137]{1,0:T(8,128)(2,1)S(1)} %copy-done.3), kind=kOutput, calls=%fused_computation.51 | convolution fusion | flops 768778240 | bytes 11260578 | tf_op jit(solution)/shard_map/dot_general | solution.py:19
  329.4 16.0 %reshape.150 = bf16[8,1280,274]{2,1,0:T(8,128)(2,1)} reshape(bf16[20480,137]{1,0:T(8,128)(2,1)} %fusion.20) | data formatting | bytes 11223040 | tf_op jit(solution)/shard_map/reshape | solution.py:20
  345.4 7.6 %select_convert_fusion = bf16[8,1280,274]{2,1,0:T(8,128)(2,1)} fusion(bf16[8,1280,274]{2,1,0:T(8,128)(2,1)} %reshape.150, pred[8,1280]{1,0:T(8,128)(4,1)S(1)} %add_compare_fusion), kind=kLoop, calls=%fused_computation | loop fusion | flops 2805760 | bytes 11233280 | tf_op jit(solution)/shard_map/convert_element_type | solution.py:21
  353.0 16.4 %fusion = bf16[1280,8,274]{0,2,1:T(8,128)(2,1)} fusion(bf16[8,1280,274]{2,1,0:T(8,128)(2,1)} %select_convert_fusion, bf16[8,1280,1280]{2,1,0:T(8,128)(2,1)} %param.12, pred[1280,8]{0,1:T(8,128)(4,1)S(1)} %broadcast_compare_fusion.1), kind=kOutput, calls=%fused_computation.4 | convolution fusion | flops 7188357120 | bytes 37447680 | tf_op jit(solution)/shard_map/snj,snc->jsc/dot_general | solution.py:41
  371.4 2.3 fusion.16
  395.3 14.4 %copy.50 = bf16[16,80,8,274]{3,2,1,0:T(8,128)(2,1)} copy(bf16[16,80,8,274]{1,3,2,0:T(8,128)(2,1)} %fusion.2) | data formatting | bytes 11223040 | tf_op jit(solution)/shard_map/stack | solution.py:43
  409.7 4.8 all-to-all-start.1
  414.5 10.1 %copy.52 = bf16[8,1280,274]{1,0,2:T(8,128)(2,1)} copy(bf16[8,1280,274]{2,1,0:T(8,128)(2,1)} %select_convert_fusion) | data formatting | bytes 11223040
  424.5 161.1 %all-to-all-done.1 = bf16[16,80,8,274]{3,2,1,0:T(8,128)(2,1)} async-done(((bf16[16,80,8,274]{3,2,1,0:T(8,128)(2,1)}), bf16[16,80,8,274]{3,2,1,0:T(8,128)(2,1)}, u32[]{:S(2)}, u32[]{:S(2)}) %all-to-all-start.1) | async-done | bytes 5611552 | tf_op jit(solution)/shard_map/all_to_all | solution.py:44
  585.6 7.9 %copy_bitcast_fusion = bf16[80,128,274]{2,1,0:T(8,128)(2,1)} fusion(bf16[16,80,8,274]{3,2,1,0:T(8,128)(2,1)} %all-to-all-done.1), kind=kLoop, calls=%fused_computation.5 | loop fusion | bytes 11223040 | tf_op jit(solution)/shard_map/reshape | solution.py:45
  593.5 10.0 %copy.53 = bf16[80,128,274]{1,0,2:T(8,128)(2,1)} copy(bf16[80,128,274]{2,1,0:T(8,128)(2,1)} %copy_bitcast_fusion) | data formatting | bytes 11223040
  (37 shorter events, 24.8 us)
Async XLA Ops:
  0.6 267.4 %copy-start = (bf16[137,137]{1,0:T(8,128)(2,1)S(1)}, bf16[137,137]{1,0:T(8,128)(2,1)}, u32[]{:S(2)}) copy-start(bf16[137,137]{1,0:T(8,128)(2,1)} %param.14) | copy-start | bytes 112618
  12.3 11.0 %copy-start.4 = (s32[1280]{0:T(1024)S(1)}, s32[1280]{0:T(1024)}, u32[]{:S(2)}) copy-start(s32[1280]{0:T(1024)} %param.10) | copy-start | bytes 15364
  33.1 6.7 %copy-start.6 = (s32[128]{0:T(128)S(1)}, s32[128]{0:T(128)}, u32[]{:S(2)}) copy-start(s32[128]{0:T(128)} %param.11) | copy-start | bytes 1540
  33.1 7.0 %copy-start.5 = (f32[137]{0:T(256)S(1)}, f32[137]{0:T(256)}, u32[]{:S(2)}) copy-start(f32[137]{0:T(256)} %param.13) | copy-start | bytes 1648
  33.1 177.8 %all-to-all-start = ((bf16[80,128,274]{2,0,1:T(8,128)(2,1)}), bf16[80,128,274]{2,0,1:T(8,128)(2,1)}, u32[]{:S(2)}, u32[]{:S(2)}) async-start(bf16[80,128,274]{2,0,1:T(8,128)(2,1)} %select_convert_fusion.1), calls=%async_computation | async-start | bytes 15728640 | tf_op jit(solution)/shard_map/all_to_all | solution.py:36
  299.7 18.9 %copy-start.3 = (bf16[137,137]{1,0:T(8,128)(2,1)S(1)}, bf16[137,137]{1,0:T(8,128)(2,1)}, u32[]{:S(2)}) copy-start(bf16[137,137]{1,0:T(8,128)(2,1)} %param.15) | copy-start | bytes 112618
  369.4 17.6 %copy-start.2 = (bf16[1280,8,274]{0,2,1:T(8,128)(2,1)S(1)}, bf16[1280,8,274]{0,2,1:T(8,128)(2,1)}, u32[]{:S(2)}) copy-start(bf16[1280,8,274]{0,2,1:T(8,128)(2,1)} %fusion) | copy-start | bytes 16834564
  409.7 175.9 %all-to-all-start.1 = ((bf16[16,80,8,274]{3,2,1,0:T(8,128)(2,1)}), bf16[16,80,8,274]{3,2,1,0:T(8,128)(2,1)}, u32[]{:S(2)}, u32[]{:S(2)}) async-start(bf16[16,80,8,274]{3,2,1,0:T(8,128)(2,1)} %copy.50), calls=%async_computation.1 | async-start | bytes 15728640 | tf_op jit(solution)/shard_map/all_to_all | solution.py:44
  585.6 17.9 %copy-start.1 = (bf16[137,137]{1,0:T(8,128)(2,1)S(1)}, bf16[137,137]{1,0:T(8,128)(2,1)}, u32[]{:S(2)}) copy-start(bf16[137,137]{1,0:T(8,128)(2,1)} %param.14) | copy-start | bytes 112618
